TPU v7x, 32 devices: a whole 2x2x4 slice. The times are simulated.
32 devices in a mesh: job: 2 (over x), tm: 2 (over core), rows: 8 (over z, y).
Axes of the slice: x: 2, y: 2, z: 4, core: 2. Of those that a mesh axis runs over, the one named last changes fastest.
Arguments:
- prior: bfloat16 [2, 524288, 64], P('tm', ('job', 'rows')), parts along dimension 1, may hold values from -80 to 80
- snapshots: bfloat16 [2, 524288, 256], P('tm', ('job', 'rows')), parts along dimension 1, may hold values from -60 to 60
Outputs:
- merged: bfloat16 [524288, 64], P(('job', 'rows'), 'tm'), parts along dimension 0
There are 2 independent parts, one for each index of `job`. A program takes and returns all parts, laid end to end along the dimension named above; each array names one. Nothing has to cross between parts.
All inputs are finite; a program needn't handle non-finite values.
Results may differ from a plain program's by a relative error of at most 0.011.
Values may be sent and summed in bfloat16 or wider, within the bound.
A program may use at most 128 MiB of HBM per device.

v0:
```python
import jax
import jax.numpy as jnp
from jax import lax
from jax.sharding import PartitionSpec as P

STEPS = 4
ITERS = 2


def partner(block, axis, bit):
    count = lax.axis_size(axis)
    route = []
    for low in range(count):
        high = low | 1 << bit
        if high != low and high < count:
            route += [(low, high), (high, low)]
    return lax.ppermute(block, axis, route)


def basis_of(gram, keep):
    order = gram.shape[0]
    basis = jnp.eye(order, keep, dtype=jnp.float32)
    for turn in range(ITERS):
        image = jnp.dot(gram, basis, precision=lax.Precision.HIGHEST)
        inner = jnp.dot(image.T, image, precision=lax.Precision.HIGHEST)
        lower = jnp.linalg.cholesky(inner)
        basis = jax.scipy.linalg.solve_triangular(lower, image.T, lower=True).T
    return basis


def project(joined, basis):
    return jnp.dot(
        joined, basis, precision=lax.Precision.HIGHEST, preferred_element_type=jnp.float32
    )


def inner_rows(left, right):
    return jnp.dot(
        left.T, right, precision=lax.Precision.HIGHEST, preferred_element_type=jnp.float32
    )


def shards(prior, snapshots):
    start_modes = prior[0]
    frames = snapshots[0]
    keep = start_modes.shape[1]
    fresh_cols = frames.shape[1] // STEPS
    whole = jnp.concatenate([start_modes, frames], axis=1)
    total = lax.psum(jnp.dot(whole.T, whole, preferred_element_type=jnp.float32), "rows")
    width = whole.shape[1]
    weights = jnp.eye(width, keep, dtype=jnp.float32)
    for step in range(STEPS):
        picker = jnp.eye(width, fresh_cols, k=-(keep + step * fresh_cols), dtype=jnp.float32)
        coeffs = jnp.concatenate([weights, picker], axis=1)
        applied = jnp.dot(total, coeffs, precision=lax.Precision.HIGHEST)
        gram = jnp.dot(coeffs.T, applied, precision=lax.Precision.HIGHEST)
        weights = jnp.dot(coeffs, basis_of(gram, keep), precision=lax.Precision.HIGHEST)
    modes = project(whole, weights)
    index = lax.axis_index("tm")
    half_keep = keep // 2
    other = partner(modes.astype(jnp.bfloat16), "tm", 0).astype(modes.dtype)
    first = jnp.where(index == 0, modes, other)
    second = jnp.where(index == 0, other, modes)
    joined = jnp.concatenate([first, second], axis=1)
    gram = lax.psum(inner_rows(joined, joined).astype(jnp.bfloat16), "rows").astype(jnp.float32)
    full_merge = project(joined, basis_of(gram, keep)).astype(jnp.bfloat16)
    merged = lax.dynamic_slice_in_dim(full_merge, index * half_keep, half_keep, 1)
    return merged


def solution(mesh):
    in_specs = (P("tm", ("job", "rows"), None), P("tm", ("job", "rows"), None))
    out_specs = P(("job", "rows"), "tm")
    return jax.shard_map(shards, mesh=mesh, in_specs=in_specs, out_specs=out_specs, check_vma=False)
```

profile of v0, /device:TPU:0, one launch (start us, length us, event | category | flops | bytes accessed | tf_op | source)
XLA Modules:
  0.0 384.0 jit_solution(9080420248376913407)
XLA Ops:
  6.5 8.5 %copy.3 = bf16[1,32768,64]{2,1,0:T(8,128)(2,1)} copy(bf16[1,32768,64]{1,2,0:T(8,128)(2,1)} %param.5) | data formatting | bytes 8388608 | tf_op args[0]
  15.0 30.9 %fusion.1 = f32[320,320]{1,0:T(8,128)} fusion(bf16[32768,256]{1,0:T(8,128)(2,1)} %bitcast.173, bf16[32768,64]{1,0:T(8,128)(2,1)} %bitcast.171), kind=kOutput, calls=%fused_computation.3 | convolution fusion | flops 6752829440 | bytes 21381120 | tf_op jit(solution)/shard_map/dot_general | solution.py:49
  46.2 75.3 %all-reduce.2.cloned.1.call-done = f32[320,320]{1,0:T(8,128)} async-done(((f32[320,320]{1,0:T(8,128)}), f32[320,320]{1,0:T(8,128)}) %all-reduce.2.cloned.1.call-update) | async-done | bytes 409616 | tf_op jit(solution)/shard_map/psum | solution.py:49
  123.9 5.8 %cholesky.164 = f32[64,64]{1,0:T(8,128)S(1)} custom-call(f32[64,64]{1,0:T(8,128)S(1)} %fusion.71), custom_call_target="Cholesky" | custom-call | tf_op jit(solution)/shard_map/jit(cholesky)/cholesky | solution.py:26
  131.1 4.9 %custom-call.14 = f32[1,64,64]{1,2,0:T(8,128)S(1)} custom-call(f32[1,64,64]{2,1,0:T(8,128)S(1)} %fusion.22), custom_call_target="InvertDiagBlocksLowerTriangular" | custom-call | tf_op jit(solution)/shard_map/jit(_solve_triangular)/triangular_solve | solution.py:27
  136.8 5.8 %cholesky.175 = f32[64,64]{1,0:T(8,128)S(1)} custom-call(f32[64,64]{1,0:T(8,128)S(1)} %fusion.67), custom_call_target="Cholesky" | custom-call | tf_op jit(solution)/shard_map/jit(cholesky)/cholesky | solution.py:26
  144.0 4.9 %custom-call.15 = f32[1,64,64]{1,2,0:T(8,128)S(1)} custom-call(f32[1,64,64]{2,1,0:T(8,128)S(1)} %fusion.23), custom_call_target="InvertDiagBlocksLowerTriangular" | custom-call | tf_op jit(solution)/shard_map/jit(_solve_triangular)/triangular_solve | solution.py:27
  149.4 1.6 fusion.13
  151.9 5.8 %cholesky.186 = f32[64,64]{1,0:T(8,128)S(1)} custom-call(f32[64,64]{1,0:T(8,128)S(1)} %fusion.63), custom_call_target="Cholesky" | custom-call | tf_op jit(solution)/shard_map/jit(cholesky)/cholesky | solution.py:26
  159.1 4.9 %custom-call.16 = f32[1,64,64]{1,2,0:T(8,128)S(1)} custom-call(f32[1,64,64]{2,1,0:T(8,128)S(1)} %fusion.24), custom_call_target="InvertDiagBlocksLowerTriangular" | custom-call | tf_op jit(solution)/shard_map/jit(_solve_triangular)/triangular_solve | solution.py:27
  164.7 5.8 %cholesky.197 = f32[64,64]{1,0:T(8,128)S(1)} custom-call(f32[64,64]{1,0:T(8,128)S(1)} %fusion.59), custom_call_target="Cholesky" | custom-call | tf_op jit(solution)/shard_map/jit(cholesky)/cholesky | solution.py:26
  171.9 4.9 %custom-call.17 = f32[1,64,64]{1,2,0:T(8,128)S(1)} custom-call(f32[1,64,64]{2,1,0:T(8,128)S(1)} %fusion.25), custom_call_target="InvertDiagBlocksLowerTriangular" | custom-call | tf_op jit(solution)/shard_map/jit(_solve_triangular)/triangular_solve | solution.py:27
  177.4 1.6 fusion.10
  179.8 6.0 %cholesky.208 = f32[64,64]{1,0:T(8,128)S(1)} custom-call(f32[64,64]{1,0:T(8,128)S(1)} %fusion.55), custom_call_target="Cholesky" | custom-call | tf_op jit(solution)/shard_map/jit(cholesky)/cholesky | solution.py:26
  187.2 4.9 %custom-call.18 = f32[1,64,64]{1,2,0:T(8,128)S(1)} custom-call(f32[1,64,64]{2,1,0:T(8,128)S(1)} %fusion.26), custom_call_target="InvertDiagBlocksLowerTriangular" | custom-call | tf_op jit(solution)/shard_map/jit(_solve_triangular)/triangular_solve | solution.py:27
  192.9 5.8 %cholesky.219 = f32[64,64]{1,0:T(8,128)S(1)} custom-call(f32[64,64]{1,0:T(8,128)S(1)} %fusion.51), custom_call_target="Cholesky" | custom-call | tf_op jit(solution)/shard_map/jit(cholesky)/cholesky | solution.py:26
  200.1 4.9 %custom-call.19 = f32[1,64,64]{1,2,0:T(8,128)S(1)} custom-call(f32[1,64,64]{2,1,0:T(8,128)S(1)} %fusion.27), custom_call_target="InvertDiagBlocksLowerTriangular" | custom-call | tf_op jit(solution)/shard_map/jit(_solve_triangular)/triangular_solve | solution.py:27
  205.5 1.6 fusion.7
  208.0 5.8 %cholesky.230 = f32[64,64]{1,0:T(8,128)S(1)} custom-call(f32[64,64]{1,0:T(8,128)S(1)} %fusion.47), custom_call_target="Cholesky" | custom-call | tf_op jit(solution)/shard_map/jit(cholesky)/cholesky | solution.py:26
  215.1 4.9 %custom-call.20 = f32[1,64,64]{1,2,0:T(8,128)S(1)} custom-call(f32[1,64,64]{2,1,0:T(8,128)S(1)} %fusion.28), custom_call_target="InvertDiagBlocksLowerTriangular" | custom-call | tf_op jit(solution)/shard_map/jit(_solve_triangular)/triangular_solve | solution.py:27
  220.8 5.8 %cholesky.241 = f32[64,64]{1,0:T(8,128)S(1)} custom-call(f32[64,64]{1,0:T(8,128)S(1)} %fusion.43), custom_call_target="Cholesky" | custom-call | tf_op jit(solution)/shard_map/jit(cholesky)/cholesky | solution.py:26
  228.0 4.9 %custom-call.21 = f32[1,64,64]{1,2,0:T(8,128)S(1)} custom-call(f32[1,64,64]{2,1,0:T(8,128)S(1)} %fusion.29), custom_call_target="InvertDiagBlocksLowerTriangular" | custom-call | tf_op jit(solution)/shard_map/jit(_solve_triangular)/triangular_solve | solution.py:27
  233.7 29.1 %fusion.90 = (bf16[32768,64]{0,1:T(8,128)(2,1)}, f32[32768,64]{0,1:T(8,128)}) fusion(f32[320,64]{1,0:T(8,128)S(1)} %fusion.5, bf16[32768,256]{1,0:T(8,128)(2,1)} %bitcast.174, bf16[32768,64]{1,0:T(8,128)(2,1)} %bitcast.172), kind=kOutput, calls=%fused_computation.150 | convolution fusion | flops 8097103872 | bytes 33636352 | tf_op jit(solution)/shard_map/dot_general | solution.py:32
  262.7 7.5 %collective-permute-done = bf16[32768,64]{0,1:T(8,128)(2,1)} collective-permute-done((bf16[32768,64]{0,1:T(8,128)(2,1)}, bf16[32768,64]{0,1:T(8,128)(2,1)}, u32[]{:S(2)}, u32[]{:S(2)}) %collective-permute-start) | collective-permute-done | bytes 4194336 | tf_op jit(solution)/shard_map/ppermute | solution.py:17
  270.2 12.1 %convert_select_fusion.1 = (f32[32768,64]{0,1:T(8,128)}, f32[32768,64]{0,1:T(8,128)}) fusion(f32[32768,64]{0,1:T(8,128)} %get-tuple-element.10, bf16[32768,64]{0,1:T(8,128)(2,1)} %collective-permute-done, pred[]{:T(512)S(6)} %eq.34), kind=kLoop, calls=%fused_computation.7 | loop fusion | flops 6291456 | bytes 29360128 | tf_op jit(solution)/shard_map/jit(_where)/select_n | solution.py:62
  282.3 18.3 %fusion.4 = bf16[128,128]{1,0:T(8,128)(2,1)S(1)} fusion(f32[32768,64]{0,1:T(8,128)} %get-tuple-element.8, f32[32768,64]{0,1:T(8,128)} %get-tuple-element.6), kind=kOutput, calls=%fused_computation.9 | convolution fusion | flops 6446661632 | bytes 16809984 | tf_op jit(solution)/shard_map/dot_general | solution.py:38
  300.6 35.4 %psum.15 = bf16[128,128]{1,0:T(8,128)(2,1)S(1)} all-reduce(bf16[128,128]{1,0:T(8,128)(2,1)S(1)} %fusion.4), channel_id=1, replica_groups=mesh['job'=2,'tm'=2,'rows'=8] {'rows'}, use_global_device_ids=true, to_apply=%region_3.6 | all-reduce | flops 16384 | bytes 65536 | tf_op jit(solution)/shard_map/psum | solution.py:65
  336.5 5.8 %cholesky.252 = f32[64,64]{1,0:T(8,128)S(1)} custom-call(f32[64,64]{1,0:T(8,128)S(1)} %fusion.39), custom_call_target="Cholesky" | custom-call | tf_op jit(solution)/shard_map/jit(cholesky)/cholesky | solution.py:26
  343.7 4.9 %custom-call.22 = f32[1,64,64]{1,2,0:T(8,128)S(1)} custom-call(f32[1,64,64]{2,1,0:T(8,128)S(1)} %fusion.30), custom_call_target="InvertDiagBlocksLowerTriangular" | custom-call | tf_op jit(solution)/shard_map/jit(_solve_triangular)/triangular_solve | solution.py:27
  349.4 5.8 %cholesky.263 = f32[64,64]{1,0:T(8,128)S(1)} custom-call(f32[64,64]{1,0:T(8,128)S(1)} %fusion.35), custom_call_target="Cholesky" | custom-call | tf_op jit(solution)/shard_map/jit(cholesky)/cholesky | solution.py:26
  356.6 4.9 %custom-call.23 = f32[1,64,64]{1,2,0:T(8,128)S(1)} custom-call(f32[1,64,64]{2,1,0:T(8,128)S(1)} %fusion.31), custom_call_target="InvertDiagBlocksLowerTriangular" | custom-call | tf_op jit(solution)/shard_map/jit(_solve_triangular)/triangular_solve | solution.py:27
  361.7 13.8 %fusion.2 = bf16[32768,64]{0,1:T(8,128)(2,1)S(1)} fusion(f32[64,128]{1,0:T(8,128)S(1)} %fusion.32, f32[32768,64]{0,1:T(8,128)} %get-tuple-element.8, f32[32768,64]{0,1:T(8,128)} %get-tuple-element.6), kind=kOutput, calls=%fused_computation.4 | convolution fusion | flops 3225419776 | bytes 21004288 | tf_op jit(solution)/shard_map/dot_general | solution.py:32
  (101 shorter events, 26.5 us)
Async XLA Ops:
  6.5 115.0 %all-reduce.2.cloned.1.call-start = ((), (), s32[]{:S(2)}) async-start(), calls=%async_computation | async-start | bytes 983040 | tf_op jit(solution)/shard_map/psum | solution.py:49
  262.7 7.5 %collective-permute-start = (bf16[32768,64]{0,1:T(8,128)(2,1)}, bf16[32768,64]{0,1:T(8,128)(2,1)}, u32[]{:S(2)}, u32[]{:S(2)}) collective-permute-start(bf16[32768,64]{0,1:T(8,128)(2,1)} %get-tuple-element.9), channel_id=1, source_target_pairs={{0,8},{8,0},{1,9},{9,1},{2,10},{10,2},{3,11},{11,3},{4,12},{12,4},... | collective-permute-start | bytes 12582920 | tf_op jit(solution)/shard_map/ppermute | solution.py:17
Sparse Core Ops, SparseCore 0:
  46.1 75.3 all-reduce.1
where the time goes:
time: 389 us; the launch traced here: 384 us
  other arithmetic  133 us (34%)
  matrix products  108 us (28%)
  waiting for transfers between devices  82.9 us (21%)
  blocking collectives  35.4 us (9%)
  between operations  14.2 us (4%)
  local copies, waits for them, and re-layouts  10.7 us (3%)
    psum x1, waiting for transfers between devices, shards(): lax.psum(jnp.dot(whole.T, whole, preferred_element_type=jnp.float32), 'ro...  75.3 us
    another operation x30, other arithmetic, basis_of(): lower = jnp.linalg.cholesky(inner)  65.4 us
    another operation x20, other arithmetic, basis_of(): basis = jax.scipy.linalg.solve_triangular(lower, image.T, lower=True).T  55.5 us
    dot_general x2, matrix products, project(): jnp.dot(joined, basis, precision=lax.Precision.HIGHEST, preferred_element...  42.9 us
    psum x1, blocking collectives, shards(): lax.psum(inner_rows(joined, joined).astype(jnp.bfloat16), 'rows')  35.4 us
    dot_general x1, matrix products, shards(): jnp.dot(whole.T, whole, preferred_element_type=jnp.float32)  30.9 us
    dot_general x1, matrix products, inner_rows(): jnp.dot(left.T, right, precision=lax.Precision.HIGHEST, preferred_element...  18.3 us
    select_n x1, other arithmetic, shards(): first = jnp.where(index == 0, modes, other)  12.1 us
  transfers between devices with their start and end apart: 2, of which 2 were waited for; matrix products, arithmetic and copies ran while one was open for 0% of the time, Pallas kernels for 0%

commit v1 on v0

--- a/solution.py
+++ b/solution.py
@@ -5,6 +5,11 @@
 
 STEPS = 4
 ITERS = 2
+
+
+def scan_the_packet(local, mesh_dim):
+    h_now = jnp.sum(lax.all_gather(local, axis_name=mesh_dim), axis=0)
+    return h_now
 
 
 def partner(block, axis, bit):
@@ -62,7 +67,9 @@
     first = jnp.where(index == 0, modes, other)
     second = jnp.where(index == 0, other, modes)
     joined = jnp.concatenate([first, second], axis=1)
-    gram = lax.psum(inner_rows(joined, joined).astype(jnp.bfloat16), "rows").astype(jnp.float32)
+    gram = scan_the_packet(inner_rows(joined, joined).astype(jnp.bfloat16), "rows").astype(
+        jnp.float32
+    )
     full_merge = project(joined, basis_of(gram, keep)).astype(jnp.bfloat16)
     merged = lax.dynamic_slice_in_dim(full_merge, index * half_keep, half_keep, 1)
     return merged

time: 389 us -> 386 us (level)
  blocking collectives: 35.4 us -> 30.8 us
    psum x1 -> x0, blocking collectives: 35.4 us -> none  [shards(): lax.psum(inner_rows(joined, joined).astype(jnp.bfloat16), 'rows')]
    all_gather x0 -> x1, blocking collectives: none -> 30.8 us  [scan_the_packet(): h_now = jnp.sum(lax.all_gather(local, axis_name=mesh_dim), axis=0)]
where the time goes in v1:
time: 386 us; the launch traced here: 380 us
  other arithmetic  133 us (34%)
  matrix products  108 us (28%)
  waiting for transfers between devices  82.8 us (21%)
  blocking collectives  30.8 us (8%)
  between operations  14.5 us (4%)
  local copies, waits for them, and re-layouts  10.7 us (3%)
    psum x1, waiting for transfers between devices, shards(): lax.psum(jnp.dot(whole.T, whole, preferred_element_type=jnp.float32), 'ro...  75.3 us
    another operation x30, other arithmetic, basis_of(): lower = jnp.linalg.cholesky(inner)  65.3 us
    another operation x20, other arithmetic, basis_of(): basis = jax.scipy.linalg.solve_triangular(lower, image.T, lower=True).T  55.5 us
    dot_general x2, matrix products, project(): jnp.dot(joined, basis, precision=lax.Precision.HIGHEST, preferred_element...  43 us
    dot_general x1, matrix products, shards(): jnp.dot(whole.T, whole, preferred_element_type=jnp.float32)  31.2 us
    all_gather x1, blocking collectives, scan_the_packet(): h_now = jnp.sum(lax.all_gather(local, axis_name=mesh_dim), axis=0)  30.8 us
    dot_general x1, matrix products, inner_rows(): jnp.dot(left.T, right, precision=lax.Precision.HIGHEST, preferred_element...  18.6 us
    select_n x1, other arithmetic, shards(): first = jnp.where(index == 0, modes, other)  12.1 us
  transfers between devices with their start and end apart: 2, of which 2 were waited for; matrix products, arithmetic and copies ran while one was open for 0% of the time, Pallas kernels for 0%

profile of v1, /device:TPU:0, one launch (start us, length us, event | category | flops | bytes accessed | tf_op | source)
XLA Modules:
  0.0 380.3 jit_solution(17910566507054814284)
XLA Ops:
  6.5 8.5 %copy.3 = bf16[1,32768,64]{2,1,0:T(8,128)(2,1)} copy(bf16[1,32768,64]{1,2,0:T(8,128)(2,1)} %param.5) | data formatting | bytes 8388608 | tf_op args[0]
  15.0 31.2 %fusion.1 = f32[320,320]{1,0:T(8,128)} fusion(bf16[32768,256]{1,0:T(8,128)(2,1)} %bitcast.175, bf16[32768,64]{1,0:T(8,128)(2,1)} %bitcast.172), kind=kOutput, calls=%fused_computation.3 | convolution fusion | flops 6752829440 | bytes 21381120 | tf_op jit(solution)/shard_map/dot_general | solution.py:54
  46.5 75.3 %all-reduce.2.cloned.1.call-done = f32[320,320]{1,0:T(8,128)} async-done(((f32[320,320]{1,0:T(8,128)}), f32[320,320]{1,0:T(8,128)}) %all-reduce.2.cloned.1.call-update) | async-done | bytes 409616 | tf_op jit(solution)/shard_map/psum | solution.py:54
  124.2 5.8 %cholesky.164 = f32[64,64]{1,0:T(8,128)S(1)} custom-call(f32[64,64]{1,0:T(8,128)S(1)} %fusion.71), custom_call_target="Cholesky" | custom-call | tf_op jit(solution)/shard_map/jit(cholesky)/cholesky | solution.py:31
  131.4 4.9 %custom-call.14 = f32[1,64,64]{1,2,0:T(8,128)S(1)} custom-call(f32[1,64,64]{2,1,0:T(8,128)S(1)} %fusion.22), custom_call_target="InvertDiagBlocksLowerTriangular" | custom-call | tf_op jit(solution)/shard_map/jit(_solve_triangular)/triangular_solve | solution.py:32
  137.1 5.8 %cholesky.175 = f32[64,64]{1,0:T(8,128)S(1)} custom-call(f32[64,64]{1,0:T(8,128)S(1)} %fusion.67), custom_call_target="Cholesky" | custom-call | tf_op jit(solution)/shard_map/jit(cholesky)/cholesky | solution.py:31
  144.3 4.9 %custom-call.15 = f32[1,64,64]{1,2,0:T(8,128)S(1)} custom-call(f32[1,64,64]{2,1,0:T(8,128)S(1)} %fusion.23), custom_call_target="InvertDiagBlocksLowerTriangular" | custom-call | tf_op jit(solution)/shard_map/jit(_solve_triangular)/triangular_solve | solution.py:32
  149.7 1.6 fusion.13
  152.2 5.8 %cholesky.186 = f32[64,64]{1,0:T(8,128)S(1)} custom-call(f32[64,64]{1,0:T(8,128)S(1)} %fusion.63), custom_call_target="Cholesky" | custom-call | tf_op jit(solution)/shard_map/jit(cholesky)/cholesky | solution.py:31
  159.4 4.9 %custom-call.16 = f32[1,64,64]{1,2,0:T(8,128)S(1)} custom-call(f32[1,64,64]{2,1,0:T(8,128)S(1)} %fusion.24), custom_call_target="InvertDiagBlocksLowerTriangular" | custom-call | tf_op jit(solution)/shard_map/jit(_solve_triangular)/triangular_solve | solution.py:32
  165.1 5.8 %cholesky.197 = f32[64,64]{1,0:T(8,128)S(1)} custom-call(f32[64,64]{1,0:T(8,128)S(1)} %fusion.59), custom_call_target="Cholesky" | custom-call | tf_op jit(solution)/shard_map/jit(cholesky)/cholesky | solution.py:31
  172.2 4.9 %custom-call.17 = f32[1,64,64]{1,2,0:T(8,128)S(1)} custom-call(f32[1,64,64]{2,1,0:T(8,128)S(1)} %fusion.25), custom_call_target="InvertDiagBlocksLowerTriangular" | custom-call | tf_op jit(solution)/shard_map/jit(_solve_triangular)/triangular_solve | solution.py:32
  177.7 1.6 fusion.10
  180.1 6.0 %cholesky.208 = f32[64,64]{1,0:T(8,128)S(1)} custom-call(f32[64,64]{1,0:T(8,128)S(1)} %fusion.55), custom_call_target="Cholesky" | custom-call | tf_op jit(solution)/shard_map/jit(cholesky)/cholesky | solution.py:31
  187.5 4.9 %custom-call.18 = f32[1,64,64]{1,2,0:T(8,128)S(1)} custom-call(f32[1,64,64]{2,1,0:T(8,128)S(1)} %fusion.26), custom_call_target="InvertDiagBlocksLowerTriangular" | custom-call | tf_op jit(solution)/shard_map/jit(_solve_triangular)/triangular_solve | solution.py:32
  193.2 5.8 %cholesky.219 = f32[64,64]{1,0:T(8,128)S(1)} custom-call(f32[64,64]{1,0:T(8,128)S(1)} %fusion.51), custom_call_target="Cholesky" | custom-call | tf_op jit(solution)/shard_map/jit(cholesky)/cholesky | solution.py:31
  200.3 4.9 %custom-call.19 = f32[1,64,64]{1,2,0:T(8,128)S(1)} custom-call(f32[1,64,64]{2,1,0:T(8,128)S(1)} %fusion.27), custom_call_target="InvertDiagBlocksLowerTriangular" | custom-call | tf_op jit(solution)/shard_map/jit(_solve_triangular)/triangular_solve | solution.py:32
  205.8 1.6 fusion.7
  208.2 5.8 %cholesky.230 = f32[64,64]{1,0:T(8,128)S(1)} custom-call(f32[64,64]{1,0:T(8,128)S(1)} %fusion.47), custom_call_target="Cholesky" | custom-call | tf_op jit(solution)/shard_map/jit(cholesky)/cholesky | solution.py:31
  215.4 4.9 %custom-call.20 = f32[1,64,64]{1,2,0:T(8,128)S(1)} custom-call(f32[1,64,64]{2,1,0:T(8,128)S(1)} %fusion.28), custom_call_target="InvertDiagBlocksLowerTriangular" | custom-call | tf_op jit(solution)/shard_map/jit(_solve_triangular)/triangular_solve | solution.py:32
  221.1 5.8 %cholesky.241 = f32[64,64]{1,0:T(8,128)S(1)} custom-call(f32[64,64]{1,0:T(8,128)S(1)} %fusion.43), custom_call_target="Cholesky" | custom-call | tf_op jit(solution)/shard_map/jit(cholesky)/cholesky | solution.py:31
  228.3 4.9 %custom-call.21 = f32[1,64,64]{1,2,0:T(8,128)S(1)} custom-call(f32[1,64,64]{2,1,0:T(8,128)S(1)} %fusion.29), custom_call_target="InvertDiagBlocksLowerTriangular" | custom-call | tf_op jit(solution)/shard_map/jit(_solve_triangular)/triangular_solve | solution.py:32
  233.9 28.9 %fusion.90 = (bf16[32768,64]{0,1:T(8,128)(2,1)}, f32[32768,64]{0,1:T(8,128)}) fusion(f32[320,64]{1,0:T(8,128)S(1)} %fusion.5, bf16[32768,256]{1,0:T(8,128)(2,1)} %bitcast.176, bf16[32768,64]{1,0:T(8,128)(2,1)} %bitcast.173), kind=kOutput, calls=%fused_computation.150 | convolution fusion | flops 8097103872 | bytes 33636352 | tf_op jit(solution)/shard_map/dot_general | solution.py:37
  262.8 7.5 %collective-permute-done = bf16[32768,64]{0,1:T(8,128)(2,1)} collective-permute-done((bf16[32768,64]{0,1:T(8,128)(2,1)}, bf16[32768,64]{0,1:T(8,128)(2,1)}, u32[]{:S(2)}, u32[]{:S(2)}) %collective-permute-start) | collective-permute-done | bytes 4194336 | tf_op jit(solution)/shard_map/ppermute | solution.py:22
  270.3 12.1 %convert_select_fusion.1 = (f32[32768,64]{0,1:T(8,128)}, f32[32768,64]{0,1:T(8,128)}) fusion(f32[32768,64]{0,1:T(8,128)} %get-tuple-element.10, bf16[32768,64]{0,1:T(8,128)(2,1)} %collective-permute-done, pred[]{:T(512)S(6)} %eq.34), kind=kLoop, calls=%fused_computation.7 | loop fusion | flops 6291456 | bytes 29360128 | tf_op jit(solution)/shard_map/jit(_where)/select_n | solution.py:67
  282.4 18.6 %fusion.4 = bf16[128,128]{1,0:T(8,128)(2,1)S(1)} fusion(f32[32768,64]{0,1:T(8,128)} %get-tuple-element.8, f32[32768,64]{0,1:T(8,128)} %get-tuple-element.6), kind=kOutput, calls=%fused_computation.9 | convolution fusion | flops 6446661632 | bytes 16809984 | tf_op jit(solution)/shard_map/dot_general | solution.py:43
  301.0 30.8 %all-gather = bf16[1024,128]{1,0:T(8,128)(2,1)S(1)} all-gather(bf16[128,128]{1,0:T(8,128)(2,1)S(1)} %fusion.4), channel_id=2, replica_groups=mesh['job'=2,'tm'=2,'rows'=8] {'rows'}, dimensions={0}, use_global_device_ids=true | all-gather | bytes 294912 | tf_op jit(solution)/shard_map/all_gather | solution.py:11
  332.3 5.8 %cholesky.252 = f32[64,64]{1,0:T(8,128)S(1)} custom-call(f32[64,64]{1,0:T(8,128)S(1)} %fusion.39), custom_call_target="Cholesky" | custom-call | tf_op jit(solution)/shard_map/jit(cholesky)/cholesky | solution.py:31
  339.4 4.9 %custom-call.22 = f32[1,64,64]{1,2,0:T(8,128)S(1)} custom-call(f32[1,64,64]{2,1,0:T(8,128)S(1)} %fusion.30), custom_call_target="InvertDiagBlocksLowerTriangular" | custom-call | tf_op jit(solution)/shard_map/jit(_solve_triangular)/triangular_solve | solution.py:32
  345.1 5.8 %cholesky.263 = f32[64,64]{1,0:T(8,128)S(1)} custom-call(f32[64,64]{1,0:T(8,128)S(1)} %fusion.35), custom_call_target="Cholesky" | custom-call | tf_op jit(solution)/shard_map/jit(cholesky)/cholesky | solution.py:31
  352.3 4.9 %custom-call.23 = f32[1,64,64]{1,2,0:T(8,128)S(1)} custom-call(f32[1,64,64]{2,1,0:T(8,128)S(1)} %fusion.31), custom_call_target="InvertDiagBlocksLowerTriangular" | custom-call | tf_op jit(solution)/shard_map/jit(_solve_triangular)/triangular_solve | solution.py:32
  357.4 14.1 %fusion.2 = bf16[32768,64]{0,1:T(8,128)(2,1)S(1)} fusion(f32[64,128]{1,0:T(8,128)S(1)} %fusion.32, f32[32768,64]{0,1:T(8,128)} %get-tuple-element.8, f32[32768,64]{0,1:T(8,128)} %get-tuple-element.6), kind=kOutput, calls=%fused_computation.4 | convolution fusion | flops 3225419776 | bytes 21004288 | tf_op jit(solution)/shard_map/dot_general | solution.py:37
  (102 shorter events, 26.5 us)
Async XLA Ops:
  6.5 115.3 %all-reduce.2.cloned.1.call-start = ((), (), s32[]{:S(2)}) async-start(), calls=%async_computation | async-start | bytes 983040 | tf_op jit(solution)/shard_map/psum | solution.py:54
  262.8 7.5 %collective-permute-start = (bf16[32768,64]{0,1:T(8,128)(2,1)}, bf16[32768,64]{0,1:T(8,128)(2,1)}, u32[]{:S(2)}, u32[]{:S(2)}) collective-permute-start(bf16[32768,64]{0,1:T(8,128)(2,1)} %get-tuple-element.9), channel_id=1, source_target_pairs={{0,8},{8,0},{1,9},{9,1},{2,10},{10,2},{3,11},{11,3},{4,12},{12,4},... | collective-permute-start | bytes 12582920 | tf_op jit(solution)/shard_map/ppermute | solution.py:22
Sparse Core Ops, SparseCore 0:
  46.4 75.3 all-reduce.1
